TPU v7x, 128 devices: a whole 4x4x4 slice. The times are simulated.
128 devices in a mesh: lon: 32 (over x, y, z_lo), dep: 4 (over z_hi, core).
Axes of the slice: x: 4, y: 4, z: 4 (z_hi: 2, z_lo: 2; z = z_hi * 2 + z_lo), core: 2. Of those that a mesh axis runs over, the one named last changes fastest.
Arguments:
- tracers: float32 [2, 80, 64, 4096], P(None, 'dep', None, 'lon'), may hold values from -6 to 6
- u_east: float32 [80, 64, 4096], P('dep', None, 'lon'), may hold values from -0.24 to 0.24
- v_north: float32 [80, 64, 4096], P('dep', None, 'lon'), may hold values from -0.24 to 0.24
- kappa_h: float32 [80, 64, 4096], P('dep', None, 'lon'), may hold values from 0.05 to 0.25
- kappa_v: float32 [80, 64, 4096], P('dep', None, 'lon'), may hold values from 0.3 to 300
- bottom: int32 [64, 4096], P(None, 'lon'), may hold values from 0 to 80
Outputs:
- tracers_out: float32 [2, 80, 64, 4096], P(None, 'dep', None, 'lon')
Inputs may be any that keep to these rules, and one draw needn't show every extreme that they name: Levels from bottom down are land; a column with 0 is all land.
All inputs are finite; a program needn't handle non-finite values.
Results may differ from a plain program's by a relative error of at most 0.0003.
Values sent between devices are 32-bit elements; how exact they have to be, the bound alone decides.
A program may use at most 128 MiB of HBM per device.

v0:
```python
import functools

import jax
import jax.numpy as jnp
from jax import lax
from jax.experimental import pallas as pl
from jax.experimental.pallas import tpu as pltpu
from jax.sharding import PartitionSpec as P

MESH = pl.DeviceIdType.MESH
SUB = 4
LAT = 64
LON = 128
THERMAL = 0.2
HALINE = 0.8
FAR = 1 << 20

(LON_R, LON_L, BOT_R, BOT_L, DG_RU, DG_RD, DG_LU, DG_LD, E_U, E_D, K_U, K_D, KX_U, KX_D, KV_U, ADV_U, ADV_D, ZM, QM, ZV, YV, XO) = range(22)
N_COPIES = 22


def lanes(shape):
    return lax.broadcasted_iota(jnp.int32, shape, len(shape) - 1)


def rows(shape):
    return lax.broadcasted_iota(jnp.int32, shape, len(shape) - 2)


def plane_shifts():
    def east(x):
        return pltpu.roll(x, LON - 1, x.ndim - 1)

    def west(x):
        return pltpu.roll(x, 1, x.ndim - 1)

    def north(x):
        return pltpu.roll(x, LAT - 1, x.ndim - 2)

    def south(x):
        return pltpu.roll(x, 1, x.ndim - 2)

    return east, west, north, south


def strip_shifts():
    def east(x):
        return pltpu.roll(x, LON - 1, x.ndim - 1)

    def west(x):
        return pltpu.roll(x, 1, x.ndim - 1)

    def north(x):
        y = pltpu.roll(x, 7, x.ndim - 2)
        return jnp.where(rows(x.shape) == 7, pltpu.roll(y, 112, x.ndim - 1), y)

    def south(x):
        y = pltpu.roll(x, 1, x.ndim - 2)
        return jnp.where(rows(x.shape) == 0, pltpu.roll(y, 16, x.ndim - 1), y)

    return east, west, north, south


def is_first_row(shape, strip):
    if strip:
        return (rows(shape) == 0) & (lanes(shape) < 16)
    return rows(shape) == 0


def is_last_row(shape, strip):
    if strip:
        return (rows(shape) == 7) & (lanes(shape) >= 112)
    return rows(shape) == LAT - 1


def upwind(c0, c1, u, v, face_x, face_y, shifts):
    east, west, north, south = shifts
    u = jnp.where(face_x, u, 0.0)
    v = jnp.where(face_y, v, 0.0)
    up = jnp.maximum(u, 0.0)
    vp = jnp.maximum(v, 0.0)
    ce = up - u
    cn = vp - v
    cw = west(up)
    cs = south(vp)
    keep = 1.0 - up - vp - west(ce) - south(cn)

    def advance(c):
        return keep * c + cw * west(c) + ce * east(c) + cs * south(c) + cn * north(c)

    for _ in range(SUB):
        c0 = advance(c0)
        c1 = advance(c1)
    return c0, c1


def fluxes(low, mid, high, kappa, mask_x, mask_y, mask_z, shifts):
    east, west, north, south = shifts
    gx = [jnp.where(mask_x, east(c) - west(c), 0.0) for c in mid]
    gy = [jnp.where(mask_y, north(c) - south(c), 0.0) for c in mid]
    gz = [jnp.where(mask_z, h - l, 0.0) for l, h in zip(low, high)]

    def density(g):
        return (-0.5 * THERMAL) * g[0] + (0.5 * HALINE) * g[1]

    rx, ry, rz = density(gx), density(gy), density(gz)
    ratio = rz / (1.0 + rx * rx + ry * ry + rz * rz)
    sx, sy = rx * ratio, ry * ratio
    sq = sx * sx + sy * sy
    flat, vert = [], []
    for n in range(2):
        fx = kappa * (gx[n] + sx * gz[n])
        fy = kappa * (gy[n] + sy * gz[n])
        vert.append(kappa * (sx * gx[n] + sy * gy[n] + sq * gz[n]))
        flat.append((east(fx) - west(fx)) + (north(fy) - south(fy)))
    return flat, vert


def pack(tiles, offset):
    group = lanes(tiles[0].shape) // 16
    out = None
    for g in range(8):
        moved = pltpu.roll(tiles[g], (16 * g + offset) % LON, tiles[g].ndim - 1)
        out = moved if out is None else jnp.where(group == g, moved, out)
    return out


def tiles_of(plane):
    return [plane[..., 8 * g : 8 * g + 8, :] for g in range(8)]


def kernel(
    n_lon, n_dep, n_lev,
    tr_hbm, u_hbm, v_hbm, kh_hbm, kv_hbm, bot_hbm,
    out_hbm,
    tr, u, v, kx, kv, bot,
    bmask, bstrip, bown, brecv,
    eown, kown, msg_r, msg_l, from_l, from_r,
    adv, flat, vert, gwin, awin, sflat, svert, edge,
    inv, gdn, rdn, rprod, pspk, qspk, fval, yend, send_end,
    zmat, qmat, qpart, zval, yval, ypart, xout, xend, tmat,
    obuf, in_sem, out_sem, ssem, rsem,
):
    lon = lax.axis_index("lon")
    dep = lax.axis_index("dep")
    right = lax.rem(lon + 1, n_lon)
    left = lax.rem(lon + n_lon - 1, n_lon)
    first = dep * n_lev
    has_up = dep > 0
    has_dn = dep < n_dep - 1
    inner = (dep == 1) | (dep == 2)
    outer = jnp.logical_not(inner)
    o_end = jnp.where(dep < 2, 0, 1)
    i_end = 1 - o_end
    out_dev = jnp.where(dep < 2, 0, 3)
    in_dev = jnp.where(dep < 2, 1, 2)
    plane = (LAT, LON)
    tile = (8, LON)

    def remote(src, dst, index, device):
        return pltpu.make_async_remote_copy(
            src_ref=src, dst_ref=dst, send_sem=ssem.at[index], recv_sem=rsem.at[index],
            device_id=device, device_id_type=MESH,
        )

    loads = [
        pltpu.make_async_copy(bot_hbm, bot, in_sem.at[0]),
        pltpu.make_async_copy(tr_hbm, tr, in_sem.at[1]),
        pltpu.make_async_copy(u_hbm, u, in_sem.at[2]),
        pltpu.make_async_copy(v_hbm, v, in_sem.at[3]),
        pltpu.make_async_copy(kh_hbm, kx.at[pl.ds(1, n_lev)], in_sem.at[4]),
        pltpu.make_async_copy(kv_hbm, kv.at[pl.ds(0, n_lev)], in_sem.at[5]),
    ]
    for copy in loads:
        copy.start()

    barrier = pltpu.get_barrier_semaphore()

    def greet(device):
        pl.semaphore_signal(barrier, inc=1, device_id=device, device_id_type=MESH)

    greet((right, dep))
    greet((left, dep))

    @pl.when(has_up)
    def _():
        greet((lon, dep - 1))
        greet((right, dep - 1))
        greet((left, dep - 1))

    @pl.when(has_dn)
    def _():
        greet((lon, dep + 1))
        greet((right, dep + 1))
        greet((left, dep + 1))

    def clear(ref, start, count):
        part = ref.at[pl.ds(start, count)]
        part[...] = jnp.zeros(part.shape, part.dtype)

    @pl.when(jnp.logical_not(has_up))
    def _():
        clear(from_l, 0, 2)
        clear(from_r, 0, 2)
        clear(eown, 0, 2)
        clear(kown, 0, 1)
        clear(kx, 0, 1)
        clear(adv, 0, 2)

    @pl.when(jnp.logical_not(has_dn))
    def _():
        clear(from_l, n_lev + 2, 2)
        clear(from_r, n_lev + 2, 2)
        clear(eown, n_lev + 2, 2)
        clear(kown, n_lev + 1, 1)
        clear(kx, n_lev + 1, 1)
        clear(adv, n_lev + 2, 2)
        clear(kv, n_lev, 1)

    clear(kown, n_lev + 2, 2)
    clear(awin, n_lev + 4, 2)

    lo8 = lanes(tile) % 16 < 8

    loads[0].wait()
    b = bot[...]
    bown[0] = pack(tiles_of(b), 8)
    bown[1] = pack(tiles_of(b), 4)
    bown[2] = pack(tiles_of(b), 12)

    def edge_masks(b, shifts, strip):
        east, west, north, south = shifts
        top = is_first_row(b.shape, strip)
        end = is_last_row(b.shape, strip)
        bn = jnp.where(end, 0, north(b))
        bs = jnp.where(top, 0, south(b))
        be, bw = east(b), west(b)
        return b, jnp.minimum(b, be), jnp.minimum(b, bn), jnp.minimum(bw, be), jnp.minimum(bs, bn)

    for i, value in enumerate(edge_masks(b, plane_shifts(), False)):
        bmask[i] = value

    for copy in loads[1:5]:
        copy.wait()
    chunk = 4
    shape = (chunk, 8, LON)

    def pack_levels(step, carry):
        at = step * chunk
        low = lanes(shape) % 16 < 8
        wl = lanes(shape) % 16

        def field(ref, offset):
            return pack([ref[pl.ds(at, chunk), 8 * g : 8 * g + 8, :] for g in range(8)], offset)

        t, s = field(tr.at[0], 8), field(tr.at[1], 8)
        uu, vv = field(u, 8), field(v, 8)
        kref = kx.at[pl.ds(1, n_lev)]
        kl, kr = field(kref, 4), field(kref, 12)
        eown[pl.ds(at + 2, chunk), 0] = t
        eown[pl.ds(at + 2, chunk), 1] = s
        eown[pl.ds(at + 2, chunk), 2] = uu
        eown[pl.ds(at + 2, chunk), 3] = vv
        kown[pl.ds(at + 1, chunk), 0] = kl
        kown[pl.ds(at + 1, chunk), 1] = kr
        msg_r[pl.ds(at, chunk), 0] = jnp.where(low, t, pltpu.roll(s, 8, 2))
        msg_r[pl.ds(at, chunk), 1] = jnp.where(
            wl == 8, pltpu.roll(kr, LON - 3, 2), jnp.where(low, uu, pltpu.roll(vv, 8, 2))
        )
        msg_l[pl.ds(at, chunk), 0] = jnp.where(low, pltpu.roll(s, LON - 8, 2), t)
        msg_l[pl.ds(at, chunk), 1] = jnp.where(
            wl == 7, pltpu.roll(kl, 3, 2), jnp.where(low, pltpu.roll(vv, LON - 8, 2), uu)
        )
        return carry

    lax.fori_loop(0, n_lev // chunk, pack_levels, 0)
    loads[5].wait()

    @pl.when(has_up & has_dn)
    def _():
        pl.semaphore_wait(barrier, 8)

    @pl.when(jnp.logical_not(has_up & has_dn))
    def _():
        pl.semaphore_wait(barrier, 5)

    top2, end2 = pl.ds(0, 2), pl.ds(n_lev - 2, 2)
    pre2, post2 = pl.ds(0, 2), pl.ds(n_lev + 2, 2)
    lon_r = remote(msg_r, from_l.at[pl.ds(2, n_lev)], LON_R, (right, dep))
    lon_l = remote(msg_l, from_r.at[pl.ds(2, n_lev)], LON_L, (left, dep))
    bot_r = remote(bown.at[0], brecv.at[0], BOT_R, (right, dep))
    bot_l = remote(bown.at[0], brecv.at[1], BOT_L, (left, dep))
    ups = [
        remote(msg_r.at[top2], from_l.at[post2], DG_RU, (right, dep - 1)),
        remote(msg_l.at[top2], from_r.at[post2], DG_LU, (left, dep - 1)),
        remote(eown.at[pl.ds(2, 2)], eown.at[post2], E_U, (lon, dep - 1)),
        remote(kown.at[1], kown.at[n_lev + 1], K_U, (lon, dep - 1)),
        remote(kx.at[1], kx.at[n_lev + 1], KX_U, (lon, dep - 1)),
        remote(kv.at[0], kv.at[n_lev], KV_U, (lon, dep - 1)),
        remote(adv.at[pl.ds(2, 2)], adv.at[post2], ADV_U, (lon, dep - 1)),
    ]
    downs = [
        remote(msg_r.at[end2], from_l.at[pre2], DG_RD, (right, dep + 1)),
        remote(msg_l.at[end2], from_r.at[pre2], DG_LD, (left, dep + 1)),
        remote(eown.at[pl.ds(n_lev, 2)], eown.at[pre2], E_D, (lon, dep + 1)),
        remote(kown.at[n_lev], kown.at[0], K_D, (lon, dep + 1)),
        remote(kx.at[n_lev], kx.at[0], KX_D, (lon, dep + 1)),
        remote(adv.at[pl.ds(n_lev, 2)], adv.at[pre2], ADV_D, (lon, dep + 1)),
    ]
    bot_r.start()
    bot_l.start()

    @pl.when(has_up)
    def _():
        for copy in ups[:-1]:
            copy.start()

    @pl.when(has_dn)
    def _():
        for copy in downs[:-1]:
            copy.start()

    lon_r.start()
    lon_l.start()

    def transport(at):
        k = first + at
        c0, c1 = upwind(
            tr[0, at], tr[1, at], u[at], v[at], bmask[1] > k, bmask[2] > k, plane_shifts()
        )
        adv[at + 2, 0] = c0
        adv[at + 2, 1] = c1

    def transport_ends(step, carry):
        transport(jnp.where(step < 2, step, step + n_lev - 4))
        return carry

    def transport_rest(step, carry):
        transport(step)
        return carry

    lax.fori_loop(0, 4, transport_ends, 0)

    @pl.when(has_up)
    def _():
        ups[-1].start()

    @pl.when(has_dn)
    def _():
        downs[-1].start()

    @pl.when(has_dn)
    def _():
        ups[5].wait_recv()

    def e_of(at):
        k = first + at
        k = jnp.where(k < 1, FAR, k)
        return jnp.where(bmask[0] > k, kv[at], 0.0)

    def eliminate(at, carry):
        ratio, prod, spike, p_top, e_here = carry
        e_next = e_of(at + 1)
        recip = 1.0 / (1.0 + e_next + e_here * (1.0 - ratio))
        gain = e_here * recip
        inv[at] = recip
        gdn[at] = gain
        rprod[at] = prod
        ratio = e_next * recip
        rdn[at] = ratio
        spike = spike * gain
        pspk[at] = spike
        p_top = p_top + prod * spike
        return ratio, prod * ratio, spike, p_top, e_next

    zero, one = jnp.zeros(plane, jnp.float32), jnp.ones(plane, jnp.float32)
    _, q_top, p_end, p_top, _ = lax.fori_loop(
        0, n_lev, eliminate, (zero, one, one, zero, e_of(0))
    )
    send_end[0, 0] = p_top
    send_end[0, 1] = p_end
    send_end[1, 0] = q_top
    send_end[1, 1] = rdn[n_lev - 1]
    z_copy = remote(send_end.at[i_end, i_end], zmat, ZM, (lon, in_dev))
    q_copy = remote(qmat, qpart, QM, (lon, 3 - dep))

    @pl.when(outer)
    def _():
        z_copy.start()

    def back_matrix(step, carry):
        p_low, q_low = carry
        at = n_lev - 1 - step
        ratio = rdn[at]
        p = pspk[at] + ratio * p_low
        q = ratio * q_low
        pspk[at] = p
        qspk[at] = q
        return p, q

    lax.fori_loop(0, n_lev, back_matrix, (zero, one))

    lax.fori_loop(2, n_lev - 2, transport_rest, 0)

    @pl.when(inner)
    def _():
        z_copy.wait_recv()
        z = zmat[...]
        inv_t = 1.0 / (1.0 - z * send_end[o_end, o_end])
        tmat[0] = inv_t
        beta = z * send_end[i_end, o_end] * inv_t
        tmat[1] = beta
        qmat[...] = send_end[i_end, i_end] + send_end[o_end, i_end] * beta
        q_copy.start()

    def flux_level(at):
        k = first + at - 1
        kw = jnp.where(k < 0, FAR, k)
        kz = jnp.where(k < 1, FAR, k + 1)
        kappa = jnp.where(bmask[0] > kw, 0.25 * kx[at], 0.0)
        f, w = fluxes(
            [adv[at, n] for n in range(2)], [adv[at + 1, n] for n in range(2)],
            [adv[at + 2, n] for n in range(2)], kappa,
            bmask[3] > kw, bmask[4] > kw, bmask[0] > kz, plane_shifts(),
        )
        for n in range(2):
            flat[at, n] = f[n]
            vert[at, n] = w[n]

    def flux_rest(step, carry):
        flux_level(step)
        return carry

    def flux_ends(step, carry):
        flux_level(jnp.where(step < 2, step, step + n_lev - 2))
        return carry

    lax.fori_loop(2, n_lev, flux_rest, 0)

    @pl.when(has_dn)
    def _():
        ups[4].wait_recv()
        ups[6].wait_recv()

    @pl.when(has_up)
    def _():
        downs[4].wait_recv()
        downs[5].wait_recv()

    lax.fori_loop(0, 4, flux_ends, 0)

    def pack_windows(step, carry):
        at = step * chunk
        low = lanes(shape) % 16 < 8
        for n in range(2):
            parts = [adv[pl.ds(at, chunk), n, 8 * g : 8 * g + 8, :] for g in range(8)]
            gwin[n, pl.ds(at, chunk)] = jnp.where(low, pack(parts, 12), pack(parts, 4))
        return carry

    lax.fori_loop(0, (n_lev + 4) // chunk, pack_windows, 0)

    bot_r.wait_recv()
    bot_l.wait_recv()
    lon_r.wait_recv()
    lon_l.wait_recv()

    @pl.when(has_dn)
    def _():
        for copy in ups[:4]:
            copy.wait_recv()

    @pl.when(has_up)
    def _():
        for copy in downs[:4]:
            copy.wait_recv()

    b_l = jnp.where(lo8, brecv[0], bown[0])
    b_r = jnp.where(lo8, bown[0], brecv[1])
    w_l = jnp.where(lo8, pltpu.roll(b_l, LON - 4, 1), bown[1])
    w_r = jnp.where(lo8, bown[2], pltpu.roll(b_r, 4, 1))
    for side, value in enumerate((b_l, b_r)):
        masks = edge_masks(value, strip_shifts(), True)
        bstrip[0, side] = masks[1]
        bstrip[1, side] = masks[2]
    for side, value in enumerate((w_l, w_r)):
        masks = edge_masks(value, strip_shifts(), True)
        bstrip[2, side] = masks[0]
        bstrip[3, side] = masks[3]
        bstrip[4, side] = masks[4]

    flatshape = (2 * chunk, 8, LON)

    def level_mask(which, start, floor, shift):
        parts = []
        for i in range(chunk):
            k = start + i
            k = jnp.where(k < floor, FAR, k + shift)
            parts.append(bstrip[which] > k)
        return jnp.concatenate(parts, axis=0)

    def join(left_part, right_part):
        return jnp.stack([left_part, right_part], axis=1).reshape(flatshape)

    def strip_transport(step, carry):
        at = step * chunk
        k = first + at - 2
        low = lanes(shape) % 16 < 8
        own = [eown[pl.ds(at, chunk), i] for i in range(4)]
        la, lb = from_l[pl.ds(at, chunk), 0], from_l[pl.ds(at, chunk), 1]
        ra, rb = from_r[pl.ds(at, chunk), 0], from_r[pl.ds(at, chunk), 1]

        def assemble(i, from_left, from_right):
            return join(jnp.where(low, from_left, own[i]), jnp.where(low, own[i], from_right))

        c0 = assemble(0, la, ra)
        c1 = assemble(1, pltpu.roll(la, LON - 8, 2), pltpu.roll(ra, 8, 2))
        uu = assemble(2, lb, rb)
        vv = assemble(3, pltpu.roll(lb, LON - 8, 2), pltpu.roll(rb, 8, 2))
        done = upwind(c0, c1, uu, vv, level_mask(0, k, 0, 0), level_mask(1, k, 0, 0), strip_shifts())
        for n in range(2):
            both = done[n].reshape(chunk, 2, 8, LON)
            g = gwin[n, pl.ds(at, chunk)]
            awin[pl.ds(at, chunk), n, 0] = jnp.where(low, pltpu.roll(both[:, 0], LON - 4, 2), g)
            awin[pl.ds(at, chunk), n, 1] = jnp.where(low, g, pltpu.roll(both[:, 1], 4, 2))
        return carry

    lax.fori_loop(0, (n_lev + 4) // chunk, strip_transport, 0)

    def strip_flux(step, carry):
        at = step * chunk
        k = first + at - 1
        wl = lanes(shape) % 16
        lb, rb = from_l[pl.ds(at + 1, chunk), 1], from_r[pl.ds(at + 1, chunk), 1]
        kl = jnp.where(wl == 3, pltpu.roll(lb, LON - 5, 2), kown[pl.ds(at, chunk), 0])
        kr = jnp.where(wl == 12, pltpu.roll(rb, 5, 2), kown[pl.ds(at, chunk), 1])
        kappa = jnp.where(level_mask(2, k, 0, 0), 0.25 * join(kl, kr), 0.0)

        def window(shift):
            return [awin[pl.ds(at + shift, chunk), n].reshape(flatshape) for n in range(2)]

        f, w = fluxes(
            window(0), window(1), window(2), kappa,
            level_mask(3, k, 0, 0), level_mask(4, k, 0, 0), level_mask(2, k, 1, 1), strip_shifts(),
        )
        for n in range(2):
            sflat[pl.ds(at, chunk), n] = f[n].reshape(chunk, 2, 8, LON)
            svert[pl.ds(at, chunk), n] = w[n].reshape(chunk, 2, 8, LON)
        return carry

    lax.fori_loop(0, (n_lev + 4) // chunk, strip_flux, 0)

    def strip_update(step, carry):
        at = step * chunk
        low = lanes(shape) % 16 < 8
        wet = level_mask(2, first + at, 0, 0)
        for n in range(2):
            gain = (
                sflat[pl.ds(at + 1, chunk), n] + svert[pl.ds(at + 2, chunk), n] - svert[pl.ds(at, chunk), n]
            ).reshape(flatshape)
            new = awin[pl.ds(at + 2, chunk), n].reshape(flatshape) + jnp.where(wet, gain, 0.0)
            both = new.reshape(chunk, 2, 8, LON)
            edge[pl.ds(at, chunk), n] = jnp.where(
                low, pltpu.roll(both[:, 1], LON - 4, 2), pltpu.roll(both[:, 0], 4, 2)
            )
        return carry

    lax.fori_loop(0, n_lev // chunk, strip_update, 0)

    yend[...] = jnp.zeros(yend.shape, jnp.float32)
    fval[0] = jnp.zeros((2,) + plane, jnp.float32)
    lane = lanes(plane)
    on_edge = (lane < 6) | (lane >= LON - 6)

    def way_down(at, carry):
        wet = bmask[0] > first + at
        scale, gain, prod = inv[at], gdn[at], rprod[at]
        for n in range(2):
            new = adv[at + 2, n] + jnp.where(wet, flat[at + 1, n] + vert[at + 2, n] - vert[at, n], 0.0)
            packed = edge[at, n]
            fixed = jnp.concatenate(
                [pltpu.roll(packed, (LON - 8 - 16 * g) % LON, 1) for g in range(8)], axis=0
            )
            new = jnp.where(on_edge, fixed, new)
            value = new * scale + gain * fval[at, n]
            fval[at + 1, n] = value
            yend[0, n] = yend[0, n] + prod * value
        return carry

    lax.fori_loop(0, n_lev, way_down, 0)
    yend[1] = fval[n_lev]

    z_val = remote(yend.at[i_end], zval, ZV, (lon, in_dev))
    y_val = remote(yval, ypart, YV, (lon, 3 - dep))
    x_val = remote(xout, xend.at[i_end], XO, (lon, out_dev))

    @pl.when(outer)
    def _():
        z_val.start()
        xend[o_end] = jnp.zeros((2,) + plane, jnp.float32)

    @pl.when(inner)
    def _():
        z_val.wait_recv()
        for n in range(2):
            alpha = (zval[n] + zmat[...] * yend[o_end, n]) * tmat[0]
            xend[o_end, n] = alpha
            yval[n] = yend[i_end, n] + send_end[o_end, i_end] * alpha
        y_val.start()

    def way_up(step, carry):
        at = n_lev - 1 - step
        ratio = rdn[at - 1]
        for n in range(2):
            fval[at, n] = fval[at, n] + ratio * fval[at + 1, n]
        return carry

    lax.fori_loop(0, n_lev - 1, way_up, 0)

    @pl.when(inner)
    def _():
        q_copy.wait_recv()
        y_val.wait_recv()
        q_other = qpart[...]
        inv_m = 1.0 / (1.0 - q_other * qmat[...])
        oo, io = send_end[o_end, o_end], send_end[i_end, o_end]
        for n in range(2):
            x_in = (ypart[n] + q_other * yval[n]) * inv_m
            xout[n] = (yend[o_end, n] + oo * zval[n] + io * x_in) * tmat[0]
            xend[i_end, n] = x_in
        x_val.start()
        for n in range(2):
            xend[o_end, n] = xend[o_end, n] + tmat[1] * xend[i_end, n]

    @pl.when(outer)
    def _():
        x_val.wait_recv()

    stores = []
    part = n_lev // 4
    for i in range(4):
        def finish(at, carry):
            p, q = pspk[at], qspk[at]
            for n in range(2):
                obuf[n, at] = fval[at + 1, n] + p * xend[0, n] + q * xend[1, n]
            return carry

        lax.fori_loop(i * part, (i + 1) * part, finish, 0)
        span = pl.ds(i * part, part)
        copy = pltpu.make_async_copy(obuf.at[:, span], out_hbm.at[:, span], out_sem.at[i])
        copy.start()
        stores.append(copy)

    for copy in (lon_r, lon_l, bot_r, bot_l):
        copy.wait_send()

    @pl.when(has_up)
    def _():
        for copy in ups:
            copy.wait_send()

    @pl.when(has_dn)
    def _():
        for copy in downs:
            copy.wait_send()

    @pl.when(outer)
    def _():
        z_copy.wait_send()
        z_val.wait_send()

    @pl.when(inner)
    def _():
        q_copy.wait_send()
        y_val.wait_send()
        x_val.wait_send()

    for copy in stores:
        copy.wait()


def per_device(n_lon, n_dep, tracers, u_east, v_north, kappa_h, kappa_v, bottom):
    n_lev = tracers.shape[1]
    ext = n_lev + 4

    def f32(*shape):
        return pltpu.VMEM(shape, jnp.float32)

    def i32(*shape):
        return pltpu.VMEM(shape, jnp.int32)

    scratch = [
        f32(2, n_lev, LAT, LON), f32(n_lev, LAT, LON), f32(n_lev, LAT, LON),
        f32(n_lev + 2, LAT, LON), f32(n_lev + 1, LAT, LON), i32(LAT, LON),
        i32(5, LAT, LON), i32(5, 2, 8, LON), i32(3, 8, LON), i32(2, 8, LON),
        f32(ext, 4, 8, LON), f32(ext, 2, 8, LON),
        f32(n_lev, 2, 8, LON), f32(n_lev, 2, 8, LON),
        f32(ext + 1, 2, 8, LON), f32(ext + 1, 2, 8, LON),
        f32(ext, 2, LAT, LON), f32(n_lev + 2, 2, LAT, LON), f32(n_lev + 2, 2, LAT, LON),
        f32(2, ext, 8, LON), f32(ext + 2, 2, 2, 8, LON),
        f32(ext, 2, 2, 8, LON), f32(ext, 2, 2, 8, LON), f32(n_lev, 2, 8, LON),
    ]
    scratch += [f32(n_lev, LAT, LON)] * 6
    scratch += [
        f32(n_lev + 1, 2, LAT, LON), f32(2, 2, LAT, LON), f32(2, 2, LAT, LON),
        f32(LAT, LON), f32(LAT, LON), f32(LAT, LON),
        f32(2, LAT, LON), f32(2, LAT, LON), f32(2, LAT, LON), f32(2, LAT, LON),
        f32(2, 2, LAT, LON), f32(2, LAT, LON),
        f32(2, n_lev, LAT, LON),
        pltpu.SemaphoreType.DMA((6,)), pltpu.SemaphoreType.DMA((4,)),
        pltpu.SemaphoreType.DMA((N_COPIES,)), pltpu.SemaphoreType.DMA((N_COPIES,)),
    ]
    hbm = pl.BlockSpec(memory_space=pl.ANY)
    return pl.pallas_call(
        functools.partial(kernel, n_lon, n_dep, n_lev),
        out_shape=jax.ShapeDtypeStruct(tracers.shape, jnp.float32),
        in_specs=[hbm] * 6,
        out_specs=hbm,
        scratch_shapes=scratch,
        name="tracer_step",
        compiler_params=pltpu.CompilerParams(
            collective_id=0, has_side_effects=True, vmem_limit_bytes=48 << 20
        ),
    )(tracers, u_east, v_north, kappa_h, kappa_v, bottom)


def solution(mesh):
    n_lon, n_dep = mesh.shape["lon"], mesh.shape["dep"]
    level = P("dep", None, "lon")
    return jax.shard_map(
        functools.partial(per_device, n_lon, n_dep),
        mesh=mesh,
        in_specs=(P(None, "dep", None, "lon"), level, level, level, level, P(None, "lon")),
        out_specs=P(None, "dep", None, "lon"),
        check_vma=False,
    )
```

profile of v0, /device:TPU:65, one launch (start us, length us, event | category | flops | bytes accessed | tf_op | source)
XLA Modules:
  0.0 47.6 jit_solution(1203686471290200691)
XLA Ops:
  0.0 0.0 copy-start
  0.0 1.3 %copy-done = f32[2,20,64,128]{3,2,1,0:T(8,128)S(1)} copy-done((f32[2,20,64,128]{3,2,1,0:T(8,128)S(1)}, f32[2,20,64,128]{3,2,1,0:T(8,128)}, u32[]{:S(2)}) %copy-start) | copy-done | bytes 1310744
  1.3 0.0 copy-start.1
  1.3 1.1 %copy-done.1 = f32[20,64,128]{2,1,0:T(8,128)S(1)} copy-done((f32[20,64,128]{2,1,0:T(8,128)S(1)}, f32[20,64,128]{2,1,0:T(8,128)}, u32[]{:S(2)}) %copy-start.1) | copy-done | bytes 655384
  2.4 0.0 copy-start.2
  2.4 1.1 %copy-done.2 = f32[20,64,128]{2,1,0:T(8,128)S(1)} copy-done((f32[20,64,128]{2,1,0:T(8,128)S(1)}, f32[20,64,128]{2,1,0:T(8,128)}, u32[]{:S(2)}) %copy-start.2) | copy-done | bytes 655384
  3.5 0.0 copy-start.3
  3.5 1.1 %copy-done.3 = f32[20,64,128]{2,1,0:T(8,128)S(1)} copy-done((f32[20,64,128]{2,1,0:T(8,128)S(1)}, f32[20,64,128]{2,1,0:T(8,128)}, u32[]{:S(2)}) %copy-start.3) | copy-done | bytes 655384
  4.6 0.0 copy-start.4
  4.6 1.1 %copy-done.4 = f32[20,64,128]{2,1,0:T(8,128)S(1)} copy-done((f32[20,64,128]{2,1,0:T(8,128)S(1)}, f32[20,64,128]{2,1,0:T(8,128)}, u32[]{:S(2)}) %copy-start.4) | copy-done | bytes 655384
  5.7 0.0 copy-start.5
  5.7 0.8 %copy-done.5 = s32[64,128]{1,0:T(8,128)S(1)} copy-done((s32[64,128]{1,0:T(8,128)S(1)}, s32[64,128]{1,0:T(8,128)}, u32[]{:S(2)}) %copy-start.5) | copy-done | bytes 32792
  6.4 40.1 %tracer_step.1 = f32[2,20,64,128]{3,2,1,0:T(8,128)S(1)} custom-call(f32[2,20,64,128]{3,2,1,0:T(8,128)S(1)} %copy-done, f32[20,64,128]{2,1,0:T(8,128)S(1)} %copy-done.1, f32[20,64,128]{2,1,0:T(8,128)S(1)} %copy-done.2, f32[20,64,128]{2,1,0:T(8,128)S(1)} %copy-done.3, f32[20,64,128]{2,1,0:T(8,128)S(1)} %copy-done.4, s32[64,128]{1,0:T(8,128)S(1)} %copy-done.5), custom_call_target="tpu_custom_call" | custom-call | tf_op jit(solution)/shard_map/tracer_step/pallas_call | solution.py:713
  46.6 1.1 %copy.8 = f32[2,20,64,128]{3,2,1,0:T(8,128)} copy(f32[2,20,64,128]{3,2,1,0:T(8,128)S(1)} %tracer_step.1) | data formatting | bytes 2621440
Async XLA Ops:
  0.0 1.3 %copy-start = (f32[2,20,64,128]{3,2,1,0:T(8,128)S(1)}, f32[2,20,64,128]{3,2,1,0:T(8,128)}, u32[]{:S(2)}) copy-start(f32[2,20,64,128]{3,2,1,0:T(8,128)} %tr_hbm.1) | copy-start | bytes 3932164
  1.3 1.1 %copy-start.1 = (f32[20,64,128]{2,1,0:T(8,128)S(1)}, f32[20,64,128]{2,1,0:T(8,128)}, u32[]{:S(2)}) copy-start(f32[20,64,128]{2,1,0:T(8,128)} %u_hbm.1) | copy-start | bytes 1966084
  2.4 1.1 %copy-start.2 = (f32[20,64,128]{2,1,0:T(8,128)S(1)}, f32[20,64,128]{2,1,0:T(8,128)}, u32[]{:S(2)}) copy-start(f32[20,64,128]{2,1,0:T(8,128)} %v_hbm.1) | copy-start | bytes 1966084
  3.5 1.1 %copy-start.3 = (f32[20,64,128]{2,1,0:T(8,128)S(1)}, f32[20,64,128]{2,1,0:T(8,128)}, u32[]{:S(2)}) copy-start(f32[20,64,128]{2,1,0:T(8,128)} %kh_hbm.1) | copy-start | bytes 1966084
  4.6 1.1 %copy-start.4 = (f32[20,64,128]{2,1,0:T(8,128)S(1)}, f32[20,64,128]{2,1,0:T(8,128)}, u32[]{:S(2)}) copy-start(f32[20,64,128]{2,1,0:T(8,128)} %kv_hbm.1) | copy-start | bytes 1966084
  5.7 0.8 %copy-start.5 = (s32[64,128]{1,0:T(8,128)S(1)}, s32[64,128]{1,0:T(8,128)}, u32[]{:S(2)}) copy-start(s32[64,128]{1,0:T(8,128)} %bot_hbm.1) | copy-start | bytes 98308
where the time goes:
time: 48 us; the launch traced here: 47.6 us
  Pallas kernels  40.1 us (84%)
  local copies, waits for them, and re-layouts  7.48 us (16%)
    pallas_call x1, Pallas kernels, per_device(): pl.pallas_call(functools.partial(kernel, n_lon, n_dep, n_lev), out_shape=...  40.1 us
    unnamed x13, local copies, waits for them, and re-layouts  7.48 us

commit v1 on v0

--- a/solution.py
+++ b/solution.py
@@ -139,7 +139,7 @@
     adv, flat, vert, gwin, awin, sflat, svert, edge,
     inv, gdn, rdn, rprod, pspk, qspk, fval, yend, send_end,
     zmat, qmat, qpart, zval, yval, ypart, xout, xend, tmat,
-    obuf, in_sem, out_sem, ssem, rsem,
+    in_sem, ssem, rsem,
 ):
     lon = lax.axis_index("lon")
     dep = lax.axis_index("dep")
@@ -242,7 +242,7 @@
 
     for copy in loads[1:5]:
         copy.wait()
-    chunk = 4
+    chunk = n_lev // 2
     shape = (chunk, 8, LON)
 
     def pack_levels(step, carry):
@@ -323,23 +323,26 @@
     lon_r.start()
     lon_l.start()
 
-    def transport(at):
-        k = first + at
-        c0, c1 = upwind(
-            tr[0, at], tr[1, at], u[at], v[at], bmask[1] > k, bmask[2] > k, plane_shifts()
-        )
-        adv[at + 2, 0] = c0
-        adv[at + 2, 1] = c1
+    batch = 4
+
+    def transport(at, count):
+        def stack(which):
+            return jnp.stack([bmask[which] > first + at + i for i in range(count)], axis=0)
+
+        span = pl.ds(at, count)
+        c0, c1 = upwind(tr[0, span], tr[1, span], u[span], v[span], stack(1), stack(2), plane_shifts())
+        adv[pl.ds(at + 2, count), 0] = c0
+        adv[pl.ds(at + 2, count), 1] = c1
 
     def transport_ends(step, carry):
-        transport(jnp.where(step < 2, step, step + n_lev - 4))
+        transport(step * (n_lev - 2), 2)
         return carry
 
     def transport_rest(step, carry):
-        transport(step)
-        return carry
-
-    lax.fori_loop(0, 4, transport_ends, 0)
+        transport(2 + step * batch, batch)
+        return carry
+
+    lax.fori_loop(0, 2, transport_ends, 0)
 
     @pl.when(has_up)
     def _():
@@ -400,7 +403,7 @@
 
     lax.fori_loop(0, n_lev, back_matrix, (zero, one))
 
-    lax.fori_loop(2, n_lev - 2, transport_rest, 0)
+    lax.fori_loop(0, (n_lev - 4) // batch, transport_rest, 0)
 
     @pl.when(inner)
     def _():
@@ -413,29 +416,33 @@
         qmat[...] = send_end[i_end, i_end] + send_end[o_end, i_end] * beta
         q_copy.start()
 
-    def flux_level(at):
-        k = first + at - 1
-        kw = jnp.where(k < 0, FAR, k)
-        kz = jnp.where(k < 1, FAR, k + 1)
-        kappa = jnp.where(bmask[0] > kw, 0.25 * kx[at], 0.0)
+    def flux_levels(at, count):
+        def stack(which, floor, shift):
+            parts = []
+            for i in range(count):
+                k = first + at + i - 1
+                parts.append(bmask[which] > jnp.where(k < floor, FAR, k + shift))
+            return jnp.stack(parts, axis=0)
+
+        kappa = jnp.where(stack(0, 0, 0), 0.25 * kx[pl.ds(at, count)], 0.0)
         f, w = fluxes(
-            [adv[at, n] for n in range(2)], [adv[at + 1, n] for n in range(2)],
-            [adv[at + 2, n] for n in range(2)], kappa,
-            bmask[3] > kw, bmask[4] > kw, bmask[0] > kz, plane_shifts(),
+            [adv[pl.ds(at, count), n] for n in range(2)], [adv[pl.ds(at + 1, count), n] for n in range(2)],
+            [adv[pl.ds(at + 2, count), n] for n in range(2)], kappa,
+            stack(3, 0, 0), stack(4, 0, 0), stack(0, 1, 1), plane_shifts(),
         )
         for n in range(2):
-            flat[at, n] = f[n]
-            vert[at, n] = w[n]
+            flat[pl.ds(at, count), n] = f[n]
+            vert[pl.ds(at, count), n] = w[n]
 
     def flux_rest(step, carry):
-        flux_level(step)
+        flux_levels(2 + 2 * step, 2)
         return carry
 
     def flux_ends(step, carry):
-        flux_level(jnp.where(step < 2, step, step + n_lev - 2))
-        return carry
-
-    lax.fori_loop(2, n_lev, flux_rest, 0)
+        flux_levels(step * n_lev, 2)
+        return carry
+
+    lax.fori_loop(0, (n_lev - 2) // 2, flux_rest, 0)
 
     @pl.when(has_dn)
     def _():
@@ -447,7 +454,10 @@
         downs[4].wait_recv()
         downs[5].wait_recv()
 
-    lax.fori_loop(0, 4, flux_ends, 0)
+    lax.fori_loop(0, 2, flux_ends, 0)
+
+    chunk = (n_lev + 4) // 2
+    shape = (chunk, 8, LON)
 
     def pack_windows(step, carry):
         at = step * chunk
@@ -549,6 +559,10 @@
 
     lax.fori_loop(0, (n_lev + 4) // chunk, strip_flux, 0)
 
+    chunk = n_lev
+    shape = (chunk, 8, LON)
+    flatshape = (2 * chunk, 8, LON)
+
     def strip_update(step, carry):
         at = step * chunk
         low = lanes(shape) % 16 < 8
@@ -571,22 +585,30 @@
     lane = lanes(plane)
     on_edge = (lane < 6) | (lane >= LON - 6)
 
-    def way_down(at, carry):
-        wet = bmask[0] > first + at
-        scale, gain, prod = inv[at], gdn[at], rprod[at]
-        for n in range(2):
-            new = adv[at + 2, n] + jnp.where(wet, flat[at + 1, n] + vert[at + 2, n] - vert[at, n], 0.0)
-            packed = edge[at, n]
-            fixed = jnp.concatenate(
-                [pltpu.roll(packed, (LON - 8 - 16 * g) % LON, 1) for g in range(8)], axis=0
-            )
-            new = jnp.where(on_edge, fixed, new)
-            value = new * scale + gain * fval[at, n]
-            fval[at + 1, n] = value
-            yend[0, n] = yend[0, n] + prod * value
-        return carry
-
-    lax.fori_loop(0, n_lev, way_down, 0)
+    group = 5
+
+    def way_down(step, carry):
+        at = step * group
+        for n in range(2):
+            value, total = fval[at, n], yend[0, n]
+            for i in range(group):
+                here = at + i
+                wet = bmask[0] > first + here
+                new = adv[here + 2, n] + jnp.where(
+                    wet, flat[here + 1, n] + vert[here + 2, n] - vert[here, n], 0.0
+                )
+                packed = edge[here, n]
+                fixed = jnp.concatenate(
+                    [pltpu.roll(packed, (LON - 8 - 16 * g) % LON, 1) for g in range(8)], axis=0
+                )
+                new = jnp.where(on_edge, fixed, new)
+                value = new * inv[here] + gdn[here] * value
+                fval[here + 1, n] = value
+                total = total + rprod[here] * value
+            yend[0, n] = total
+        return carry
+
+    lax.fori_loop(0, n_lev // group, way_down, 0)
     yend[1] = fval[n_lev]
 
     z_val = remote(yend.at[i_end], zval, ZV, (lon, in_dev))
@@ -635,20 +657,15 @@
     def _():
         x_val.wait_recv()
 
-    stores = []
     part = n_lev // 4
     for i in range(4):
         def finish(at, carry):
             p, q = pspk[at], qspk[at]
             for n in range(2):
-                obuf[n, at] = fval[at + 1, n] + p * xend[0, n] + q * xend[1, n]
+                out_hbm[n, at] = fval[at + 1, n] + p * xend[0, n] + q * xend[1, n]
             return carry
 
         lax.fori_loop(i * part, (i + 1) * part, finish, 0)
-        span = pl.ds(i * part, part)
-        copy = pltpu.make_async_copy(obuf.at[:, span], out_hbm.at[:, span], out_sem.at[i])
-        copy.start()
-        stores.append(copy)
 
     for copy in (lon_r, lon_l, bot_r, bot_l):
         copy.wait_send()
@@ -673,9 +690,6 @@
         q_copy.wait_send()
         y_val.wait_send()
         x_val.wait_send()
-
-    for copy in stores:
-        copy.wait()
 
 
 def per_device(n_lon, n_dep, tracers, u_east, v_north, kappa_h, kappa_v, bottom):
@@ -705,22 +719,21 @@
         f32(LAT, LON), f32(LAT, LON), f32(LAT, LON),
         f32(2, LAT, LON), f32(2, LAT, LON), f32(2, LAT, LON), f32(2, LAT, LON),
         f32(2, 2, LAT, LON), f32(2, LAT, LON),
-        f32(2, n_lev, LAT, LON),
-        pltpu.SemaphoreType.DMA((6,)), pltpu.SemaphoreType.DMA((4,)),
+        pltpu.SemaphoreType.DMA((6,)),
         pltpu.SemaphoreType.DMA((N_COPIES,)), pltpu.SemaphoreType.DMA((N_COPIES,)),
     ]
-    hbm = pl.BlockSpec(memory_space=pl.ANY)
+    hbm = pl.BlockSpec(memory_space=pltpu.HBM)
     return pl.pallas_call(
         functools.partial(kernel, n_lon, n_dep, n_lev),
         out_shape=jax.ShapeDtypeStruct(tracers.shape, jnp.float32),
         in_specs=[hbm] * 6,
-        out_specs=hbm,
+        out_specs=pl.BlockSpec(memory_space=pltpu.VMEM),
         scratch_shapes=scratch,
         name="tracer_step",
         compiler_params=pltpu.CompilerParams(
             collective_id=0, has_side_effects=True, vmem_limit_bytes=48 << 20
         ),
-    )(tracers, u_east, v_north, kappa_h, kappa_v, bottom)
+    )(*(pltpu.with_memory_space_constraint(a, pltpu.HBM) for a in (tracers, u_east, v_north, kappa_h, kappa_v, bottom)))
 
 
 def solution(mesh):

time: 48 us -> 33.5 us (0.70)
  Pallas kernels: 40.1 us -> 32.4 us
  local copies, waits for them, and re-layouts: 7.48 us -> 1.06 us
    pallas_call x1, Pallas kernels: 40.1 us -> 32.4 us  [per_device(): pl.pallas_call(functools.partial(kernel, n_lon, n_dep, n_lev), out_shape=...]
    unnamed x13 -> x1, local copies, waits for them, and re-layouts: 7.48 us -> 1.06 us
where the time goes in v1:
time: 33.5 us; the launch traced here: 33.4 us
  Pallas kernels  32.4 us (97%)
  local copies, waits for them, and re-layouts  1.06 us (3%)
    pallas_call x1, Pallas kernels, per_device(): pl.pallas_call(functools.partial(kernel, n_lon, n_dep, n_lev), out_shape=...  32.4 us
    unnamed x1, local copies, waits for them, and re-layouts  1.06 us

profile of v1, /device:TPU:65, one launch (start us, length us, event | category | flops | bytes accessed | tf_op | source)
XLA Modules:
  0.0 33.4 jit_solution(6125775998984502581)
XLA Ops:
  0.0 32.4 %tracer_step.1 = f32[2,20,64,128]{3,2,1,0:T(8,128)S(1)} custom-call(f32[2,20,64,128]{3,2,1,0:T(8,128)} %tr_hbm.1, f32[20,64,128]{2,1,0:T(8,128)} %u_hbm.1, f32[20,64,128]{2,1,0:T(8,128)} %v_hbm.1, f32[20,64,128]{2,1,0:T(8,128)} %kh_hbm.1, f32[20,64,128]{2,1,0:T(8,128)} %kv_hbm.1, s32[64,128]{1,0:T(8,128)} %bot_hbm.1), custom_call_target="tpu_custom_call" | custom-call | tf_op jit(solution)/shard_map/tracer_step/pallas_call | solution.py:726
  32.4 1.1 %copy.8 = f32[2,20,64,128]{3,2,1,0:T(8,128)} copy(f32[2,20,64,128]{3,2,1,0:T(8,128)S(1)} %tracer_step.1) | data formatting | bytes 2621440

commit v2 on v1

--- a/solution.py
+++ b/solution.py
@@ -14,6 +14,7 @@
 THERMAL = 0.2
 HALINE = 0.8
 FAR = 1 << 20
+TB, FB, SC = 4, 2, 12
 
 (LON_R, LON_L, BOT_R, BOT_L, DG_RU, DG_RD, DG_LU, DG_LD, E_U, E_D, K_U, K_D, KX_U, KX_D, KV_U, ADV_U, ADV_D, ZM, QM, ZV, YV, XO) = range(22)
 N_COPIES = 22
@@ -100,18 +101,14 @@
     gy = [jnp.where(mask_y, north(c) - south(c), 0.0) for c in mid]
     gz = [jnp.where(mask_z, h - l, 0.0) for l, h in zip(low, high)]
 
-    def density(g):
-        return (-0.5 * THERMAL) * g[0] + (0.5 * HALINE) * g[1]
-
-    rx, ry, rz = density(gx), density(gy), density(gz)
-    ratio = rz / (1.0 + rx * rx + ry * ry + rz * rz)
+    rx, ry, rz = (g[1] - (THERMAL / HALINE) * g[0] for g in (gx, gy, gz))
+    ratio = rz / ((4.0 / HALINE**2) + rx * rx + ry * ry + rz * rz)
     sx, sy = rx * ratio, ry * ratio
-    sq = sx * sx + sy * sy
     flat, vert = [], []
     for n in range(2):
         fx = kappa * (gx[n] + sx * gz[n])
         fy = kappa * (gy[n] + sy * gz[n])
-        vert.append(kappa * (sx * gx[n] + sy * gy[n] + sq * gz[n]))
+        vert.append(sx * fx + sy * fy)
         flat.append((east(fx) - west(fx)) + (north(fy) - south(fy)))
     return flat, vert
 
@@ -265,15 +262,25 @@
         kown[pl.ds(at + 1, chunk), 1] = kr
         msg_r[pl.ds(at, chunk), 0] = jnp.where(low, t, pltpu.roll(s, 8, 2))
         msg_r[pl.ds(at, chunk), 1] = jnp.where(
-            wl == 8, pltpu.roll(kr, LON - 3, 2), jnp.where(low, uu, pltpu.roll(vv, 8, 2))
+            wl == 10, pltpu.roll(kr, LON - 1, 2), jnp.where(low, uu, pltpu.roll(vv, 8, 2))
         )
         msg_l[pl.ds(at, chunk), 0] = jnp.where(low, pltpu.roll(s, LON - 8, 2), t)
         msg_l[pl.ds(at, chunk), 1] = jnp.where(
-            wl == 7, pltpu.roll(kl, 3, 2), jnp.where(low, pltpu.roll(vv, LON - 8, 2), uu)
+            wl == 5, pltpu.roll(kl, 1, 2), jnp.where(low, pltpu.roll(vv, LON - 8, 2), uu)
         )
         return carry
 
     lax.fori_loop(0, n_lev // chunk, pack_levels, 0)
+
+    guests = n_lev // 4
+    hosts = n_lev - guests
+    slot = lanes((guests, 8, LON)) % 8
+    for i in range(2):
+        guest_r, guest_l = msg_r[pl.ds(hosts, guests), i], msg_l[pl.ds(hosts, guests), i]
+        for j in range(3):
+            span = pl.ds(j * guests, guests)
+            msg_r[span, i] = jnp.where(slot < 2, pltpu.roll(guest_r, LON - 2 - 2 * j, 2), msg_r[span, i])
+            msg_l[span, i] = jnp.where(slot >= 6, pltpu.roll(guest_l, 6 - 2 * j, 2), msg_l[span, i])
     loads[5].wait()
 
     @pl.when(has_up & has_dn)
@@ -286,8 +293,8 @@
 
     top2, end2 = pl.ds(0, 2), pl.ds(n_lev - 2, 2)
     pre2, post2 = pl.ds(0, 2), pl.ds(n_lev + 2, 2)
-    lon_r = remote(msg_r, from_l.at[pl.ds(2, n_lev)], LON_R, (right, dep))
-    lon_l = remote(msg_l, from_r.at[pl.ds(2, n_lev)], LON_L, (left, dep))
+    lon_r = remote(msg_r.at[pl.ds(0, hosts)], from_l.at[pl.ds(2, hosts)], LON_R, (right, dep))
+    lon_l = remote(msg_l.at[pl.ds(0, hosts)], from_r.at[pl.ds(2, hosts)], LON_L, (left, dep))
     bot_r = remote(bown.at[0], brecv.at[0], BOT_R, (right, dep))
     bot_l = remote(bown.at[0], brecv.at[1], BOT_L, (left, dep))
     ups = [
@@ -323,7 +330,7 @@
     lon_r.start()
     lon_l.start()
 
-    batch = 4
+    batch = TB
 
     def transport(at, count):
         def stack(which):
@@ -351,6 +358,36 @@
     @pl.when(has_dn)
     def _():
         downs[-1].start()
+
+    lax.fori_loop(0, (n_lev - 4) // batch, transport_rest, 0)
+
+    def flux_levels(at, count):
+        def stack(which, floor, shift):
+            parts = []
+            for i in range(count):
+                k = first + at + i - 1
+                parts.append(bmask[which] > jnp.where(k < floor, FAR, k + shift))
+            return jnp.stack(parts, axis=0)
+
+        kappa = jnp.where(stack(0, 0, 0), 0.25 * kx[pl.ds(at, count)], 0.0)
+        f, w = fluxes(
+            [adv[pl.ds(at, count), n] for n in range(2)], [adv[pl.ds(at + 1, count), n] for n in range(2)],
+            [adv[pl.ds(at + 2, count), n] for n in range(2)], kappa,
+            stack(3, 0, 0), stack(4, 0, 0), stack(0, 1, 1), plane_shifts(),
+        )
+        for n in range(2):
+            flat[pl.ds(at, count), n] = f[n]
+            vert[pl.ds(at, count), n] = w[n]
+
+    def flux_rest(step, carry):
+        flux_levels(2 + FB * step, FB)
+        return carry
+
+    def flux_ends(step, carry):
+        flux_levels(step * n_lev, 2)
+        return carry
+
+    lax.fori_loop(0, (n_lev - 2) // FB, flux_rest, 0)
 
     @pl.when(has_dn)
     def _():
@@ -403,7 +440,17 @@
 
     lax.fori_loop(0, n_lev, back_matrix, (zero, one))
 
-    lax.fori_loop(0, (n_lev - 4) // batch, transport_rest, 0)
+    @pl.when(has_dn)
+    def _():
+        ups[4].wait_recv()
+        ups[6].wait_recv()
+
+    @pl.when(has_up)
+    def _():
+        downs[4].wait_recv()
+        downs[5].wait_recv()
+
+    lax.fori_loop(0, 2, flux_ends, 0)
 
     @pl.when(inner)
     def _():
@@ -416,47 +463,7 @@
         qmat[...] = send_end[i_end, i_end] + send_end[o_end, i_end] * beta
         q_copy.start()
 
-    def flux_levels(at, count):
-        def stack(which, floor, shift):
-            parts = []
-            for i in range(count):
-                k = first + at + i - 1
-                parts.append(bmask[which] > jnp.where(k < floor, FAR, k + shift))
-            return jnp.stack(parts, axis=0)
-
-        kappa = jnp.where(stack(0, 0, 0), 0.25 * kx[pl.ds(at, count)], 0.0)
-        f, w = fluxes(
-            [adv[pl.ds(at, count), n] for n in range(2)], [adv[pl.ds(at + 1, count), n] for n in range(2)],
-            [adv[pl.ds(at + 2, count), n] for n in range(2)], kappa,
-            stack(3, 0, 0), stack(4, 0, 0), stack(0, 1, 1), plane_shifts(),
-        )
-        for n in range(2):
-            flat[pl.ds(at, count), n] = f[n]
-            vert[pl.ds(at, count), n] = w[n]
-
-    def flux_rest(step, carry):
-        flux_levels(2 + 2 * step, 2)
-        return carry
-
-    def flux_ends(step, carry):
-        flux_levels(step * n_lev, 2)
-        return carry
-
-    lax.fori_loop(0, (n_lev - 2) // 2, flux_rest, 0)
-
-    @pl.when(has_dn)
-    def _():
-        ups[4].wait_recv()
-        ups[6].wait_recv()
-
-    @pl.when(has_up)
-    def _():
-        downs[4].wait_recv()
-        downs[5].wait_recv()
-
-    lax.fori_loop(0, 2, flux_ends, 0)
-
-    chunk = (n_lev + 4) // 2
+    chunk = SC
     shape = (chunk, 8, LON)
 
     def pack_windows(step, carry):
@@ -473,6 +480,16 @@
     bot_l.wait_recv()
     lon_r.wait_recv()
     lon_l.wait_recv()
+    for i in range(2):
+        guest_l = guest_r = None
+        for j in range(3):
+            span = pl.ds(2 + j * guests, guests)
+            part_l = pltpu.roll(from_l[span, i], 2 + 2 * j, 2)
+            part_r = pltpu.roll(from_r[span, i], LON - 6 + 2 * j, 2)
+            guest_l = part_l if j == 0 else jnp.where(slot >= 2 + 2 * j, part_l, guest_l)
+            guest_r = part_r if j == 0 else jnp.where(slot >= 2 * j, part_r, guest_r)
+        from_l[pl.ds(2 + hosts, guests), i] = guest_l
+        from_r[pl.ds(2 + hosts, guests), i] = guest_r
 
     @pl.when(has_dn)
     def _():
@@ -541,8 +558,8 @@
         k = first + at - 1
         wl = lanes(shape) % 16
         lb, rb = from_l[pl.ds(at + 1, chunk), 1], from_r[pl.ds(at + 1, chunk), 1]
-        kl = jnp.where(wl == 3, pltpu.roll(lb, LON - 5, 2), kown[pl.ds(at, chunk), 0])
-        kr = jnp.where(wl == 12, pltpu.roll(rb, 5, 2), kown[pl.ds(at, chunk), 1])
+        kl = jnp.where(wl == 3, pltpu.roll(lb, LON - 7, 2), kown[pl.ds(at, chunk), 0])
+        kr = jnp.where(wl == 12, pltpu.roll(rb, 7, 2), kown[pl.ds(at, chunk), 1])
         kappa = jnp.where(level_mask(2, k, 0, 0), 0.25 * join(kl, kr), 0.0)
 
         def window(shift):

time: 33.5 us -> 31.1 us (0.928)
  the two profiles are of different devices: /device:TPU:65 before, /device:TPU:1 now
where the time goes in v2:
time: 31.1 us; the launch traced here: 31 us
  Pallas kernels  29.9 us (96%)
  local copies, waits for them, and re-layouts  1.06 us (3%)
    pallas_call x1, Pallas kernels, per_device(): pl.pallas_call(functools.partial(kernel, n_lon, n_dep, n_lev), out_shape=...  29.9 us
    unnamed x1, local copies, waits for them, and re-layouts  1.06 us

profile of v2, /device:TPU:1, one launch (start us, length us, event | category | flops | bytes accessed | tf_op | source)
XLA Modules:
  0.0 31.0 jit_solution(15824387074547268650)
XLA Ops:
  0.0 29.9 %tracer_step.1 = f32[2,20,64,128]{3,2,1,0:T(8,128)S(1)} custom-call(f32[2,20,64,128]{3,2,1,0:T(8,128)} %tr_hbm.1, f32[20,64,128]{2,1,0:T(8,128)} %u_hbm.1, f32[20,64,128]{2,1,0:T(8,128)} %v_hbm.1, f32[20,64,128]{2,1,0:T(8,128)} %kh_hbm.1, f32[20,64,128]{2,1,0:T(8,128)} %kv_hbm.1, s32[64,128]{1,0:T(8,128)} %bot_hbm.1), custom_call_target="tpu_custom_call" | custom-call | tf_op jit(solution)/shard_map/tracer_step/pallas_call | solution.py:743
  29.9 1.1 %copy.8 = f32[2,20,64,128]{3,2,1,0:T(8,128)} copy(f32[2,20,64,128]{3,2,1,0:T(8,128)S(1)} %tracer_step.1) | data formatting | bytes 2621440

commit v3 on v0

--- a/solution.py
+++ b/solution.py
@@ -14,9 +14,11 @@
 THERMAL = 0.2
 HALINE = 0.8
 FAR = 1 << 20
-
-(LON_R, LON_L, BOT_R, BOT_L, DG_RU, DG_RD, DG_LU, DG_LD, E_U, E_D, K_U, K_D, KX_U, KX_D, KV_U, ADV_U, ADV_D, ZM, QM, ZV, YV, XO) = range(22)
-N_COPIES = 22
+TB, FB, FC, NQ = 8, 2, 12, 2
+
+(LON_R, LON_L, BOT_R, BOT_L, DG_RU, DG_RD, DG_LU, DG_LD, E_U, E_D, K_U, K_D, KX_U, KX_D, KV_U, ADV_U, ADV_D, ZM, QM) = range(19)
+ZV, YV, XO, LON2 = 19, 21, 23, 25
+N_COPIES = 27
 
 
 def lanes(shape):
@@ -94,26 +96,27 @@
     return c0, c1
 
 
-def fluxes(low, mid, high, kappa, mask_x, mask_y, mask_z, shifts):
-    east, west, north, south = shifts
+def fluxes(low, mid, high, north, south, kappa, mask_x, mask_y, mask_z):
+    def east(x):
+        return pltpu.roll(x, LON - 1, x.ndim - 1)
+
+    def west(x):
+        return pltpu.roll(x, 1, x.ndim - 1)
+
     gx = [jnp.where(mask_x, east(c) - west(c), 0.0) for c in mid]
-    gy = [jnp.where(mask_y, north(c) - south(c), 0.0) for c in mid]
-    gz = [jnp.where(mask_z, h - l, 0.0) for l, h in zip(low, high)]
-
-    def density(g):
-        return (-0.5 * THERMAL) * g[0] + (0.5 * HALINE) * g[1]
-
-    rx, ry, rz = density(gx), density(gy), density(gz)
-    ratio = rz / (1.0 + rx * rx + ry * ry + rz * rz)
+    gy = [jnp.where(mask_y, a - b, 0.0) for a, b in zip(north, south)]
+    gz = [jnp.where(mask_z, a - b, 0.0) for a, b in zip(high, low)]
+    rx, ry, rz = (g[1] - (THERMAL / HALINE) * g[0] for g in (gx, gy, gz))
+    ratio = rz / ((4.0 / HALINE**2) + rx * rx + ry * ry + rz * rz)
     sx, sy = rx * ratio, ry * ratio
-    sq = sx * sx + sy * sy
-    flat, vert = [], []
+    flat, side, vert = [], [], []
     for n in range(2):
         fx = kappa * (gx[n] + sx * gz[n])
         fy = kappa * (gy[n] + sy * gz[n])
-        vert.append(kappa * (sx * gx[n] + sy * gy[n] + sq * gz[n]))
-        flat.append((east(fx) - west(fx)) + (north(fy) - south(fy)))
-    return flat, vert
+        vert.append(sx * fx + sy * fy)
+        flat.append(east(fx) - west(fx))
+        side.append(fy)
+    return flat, side, vert
 
 
 def pack(tiles, offset):
@@ -139,7 +142,7 @@
     adv, flat, vert, gwin, awin, sflat, svert, edge,
     inv, gdn, rdn, rprod, pspk, qspk, fval, yend, send_end,
     zmat, qmat, qpart, zval, yval, ypart, xout, xend, tmat,
-    obuf, in_sem, out_sem, ssem, rsem,
+    in_sem, ssem, rsem,
 ):
     lon = lax.axis_index("lon")
     dep = lax.axis_index("dep")
@@ -163,16 +166,22 @@
             device_id=device, device_id_type=MESH,
         )
 
-    loads = [
-        pltpu.make_async_copy(bot_hbm, bot, in_sem.at[0]),
-        pltpu.make_async_copy(tr_hbm, tr, in_sem.at[1]),
-        pltpu.make_async_copy(u_hbm, u, in_sem.at[2]),
-        pltpu.make_async_copy(v_hbm, v, in_sem.at[3]),
-        pltpu.make_async_copy(kh_hbm, kx.at[pl.ds(1, n_lev)], in_sem.at[4]),
-        pltpu.make_async_copy(kv_hbm, kv.at[pl.ds(0, n_lev)], in_sem.at[5]),
-    ]
-    for copy in loads:
-        copy.start()
+    part = n_lev // NQ
+    load_bot = pltpu.make_async_copy(bot_hbm, bot, in_sem.at[0])
+    load_kv = pltpu.make_async_copy(kv_hbm, kv.at[pl.ds(0, n_lev)], in_sem.at[1])
+    load_bot.start()
+    loads = []
+    for i in range(NQ):
+        span = pl.ds(i * part, part)
+        loads.append([
+            pltpu.make_async_copy(tr_hbm.at[:, span], tr.at[:, span], in_sem.at[4 * i + 2]),
+            pltpu.make_async_copy(u_hbm.at[span], u.at[span], in_sem.at[4 * i + 3]),
+            pltpu.make_async_copy(v_hbm.at[span], v.at[span], in_sem.at[4 * i + 4]),
+            pltpu.make_async_copy(kh_hbm.at[span], kx.at[pl.ds(1 + i * part, part)], in_sem.at[4 * i + 5]),
+        ])
+        for copy in loads[-1]:
+            copy.start()
+    load_kv.start()
 
     barrier = pltpu.get_barrier_semaphore()
 
@@ -222,7 +231,7 @@
 
     lo8 = lanes(tile) % 16 < 8
 
-    loads[0].wait()
+    load_bot.wait()
     b = bot[...]
     bown[0] = pack(tiles_of(b), 8)
     bown[1] = pack(tiles_of(b), 4)
@@ -240,9 +249,7 @@
     for i, value in enumerate(edge_masks(b, plane_shifts(), False)):
         bmask[i] = value
 
-    for copy in loads[1:5]:
-        copy.wait()
-    chunk = 4
+    chunk = part
     shape = (chunk, 8, LON)
 
     def pack_levels(step, carry):
@@ -265,16 +272,50 @@
         kown[pl.ds(at + 1, chunk), 1] = kr
         msg_r[pl.ds(at, chunk), 0] = jnp.where(low, t, pltpu.roll(s, 8, 2))
         msg_r[pl.ds(at, chunk), 1] = jnp.where(
-            wl == 8, pltpu.roll(kr, LON - 3, 2), jnp.where(low, uu, pltpu.roll(vv, 8, 2))
+            wl == 10, pltpu.roll(kr, LON - 1, 2), jnp.where(low, uu, pltpu.roll(vv, 8, 2))
         )
         msg_l[pl.ds(at, chunk), 0] = jnp.where(low, pltpu.roll(s, LON - 8, 2), t)
         msg_l[pl.ds(at, chunk), 1] = jnp.where(
-            wl == 7, pltpu.roll(kl, 3, 2), jnp.where(low, pltpu.roll(vv, LON - 8, 2), uu)
+            wl == 5, pltpu.roll(kl, 1, 2), jnp.where(low, pltpu.roll(vv, LON - 8, 2), uu)
         )
         return carry
 
-    lax.fori_loop(0, n_lev // chunk, pack_levels, 0)
-    loads[5].wait()
+    for i in range(NQ):
+        for copy in loads[i]:
+            copy.wait()
+        pack_levels(i, 0)
+
+    guests = n_lev // 4
+    hosts = n_lev - guests
+    slot = lanes((guests, 8, LON)) % 8
+    for i in range(2):
+        guest_r, guest_l = msg_r[pl.ds(hosts, guests), i], msg_l[pl.ds(hosts, guests), i]
+        for j in range(3):
+            span = pl.ds(j * guests, guests)
+            msg_r[span, i] = jnp.where(slot < 2, pltpu.roll(guest_r, LON - 2 - 2 * j, 2), msg_r[span, i])
+            msg_l[span, i] = jnp.where(slot >= 6, pltpu.roll(guest_l, 6 - 2 * j, 2), msg_l[span, i])
+    load_kv.wait()
+
+    batch = TB
+
+    def transport(at, count):
+        def stack(which):
+            return jnp.stack([bmask[which] > first + at + i for i in range(count)], axis=0)
+
+        span = pl.ds(at, count)
+        c0, c1 = upwind(tr[0, span], tr[1, span], u[span], v[span], stack(1), stack(2), plane_shifts())
+        adv[pl.ds(at + 2, count), 0] = c0
+        adv[pl.ds(at + 2, count), 1] = c1
+
+    def transport_ends(step, carry):
+        transport(step * (n_lev - 2), 2)
+        return carry
+
+    def transport_rest(step, carry):
+        transport(2 + step * batch, batch)
+        return carry
+
+    lax.fori_loop(0, 2, transport_ends, 0)
 
     @pl.when(has_up & has_dn)
     def _():
@@ -286,8 +327,21 @@
 
     top2, end2 = pl.ds(0, 2), pl.ds(n_lev - 2, 2)
     pre2, post2 = pl.ds(0, 2), pl.ds(n_lev + 2, 2)
-    lon_r = remote(msg_r, from_l.at[pl.ds(2, n_lev)], LON_R, (right, dep))
-    lon_l = remote(msg_l, from_r.at[pl.ds(2, n_lev)], LON_L, (left, dep))
+    early = (n_lev + 4) // 2 - 2
+    first_part, second_part = (0, early), (early, hosts - early)
+
+    def lon_copy(message, target, part, index, device):
+        start, count = part
+        return remote(message.at[pl.ds(start, count)], target.at[pl.ds(2 + start, count)], index, device)
+
+    lon_1 = [
+        lon_copy(msg_r, from_l, first_part, LON_R, (right, dep)),
+        lon_copy(msg_l, from_r, first_part, LON_L, (left, dep)),
+    ]
+    lon_2 = [
+        lon_copy(msg_r, from_l, second_part, LON2, (right, dep)),
+        lon_copy(msg_l, from_r, second_part, LON2 + 1, (left, dep)),
+    ]
     bot_r = remote(bown.at[0], brecv.at[0], BOT_R, (right, dep))
     bot_l = remote(bown.at[0], brecv.at[1], BOT_L, (left, dep))
     ups = [
@@ -307,47 +361,69 @@
         remote(kx.at[n_lev], kx.at[0], KX_D, (lon, dep + 1)),
         remote(adv.at[pl.ds(n_lev, 2)], adv.at[pre2], ADV_D, (lon, dep + 1)),
     ]
+    for copy in lon_1:
+        copy.start()
     bot_r.start()
     bot_l.start()
 
     @pl.when(has_up)
     def _():
-        for copy in ups[:-1]:
+        for copy in ups[:4] + ups[5:6]:
             copy.start()
 
     @pl.when(has_dn)
     def _():
-        for copy in downs[:-1]:
+        for copy in downs[:4]:
             copy.start()
 
-    lon_r.start()
-    lon_l.start()
-
-    def transport(at):
-        k = first + at
-        c0, c1 = upwind(
-            tr[0, at], tr[1, at], u[at], v[at], bmask[1] > k, bmask[2] > k, plane_shifts()
-        )
-        adv[at + 2, 0] = c0
-        adv[at + 2, 1] = c1
-
-    def transport_ends(step, carry):
-        transport(jnp.where(step < 2, step, step + n_lev - 4))
-        return carry
-
-    def transport_rest(step, carry):
-        transport(step)
-        return carry
-
-    lax.fori_loop(0, 4, transport_ends, 0)
+    for copy in lon_2:
+        copy.start()
+
+    lax.fori_loop(0, (n_lev - 4) // batch, transport_rest, 0)
 
     @pl.when(has_up)
     def _():
-        ups[-1].start()
+        ups[6].start()
+        ups[4].start()
 
     @pl.when(has_dn)
     def _():
-        downs[-1].start()
+        downs[5].start()
+        downs[4].start()
+
+
+    def flux_levels(at, count):
+        _, _, north, south = plane_shifts()
+        for i in [at + i for i in range(count)]:
+            k = first + i - 1
+            kw = jnp.where(k < 0, FAR, k)
+            kz = jnp.where(k < 1, FAR, k + 1)
+            mid = [adv[i + 1, n] for n in range(2)]
+            norths, souths = [north(c) for c in mid], [south(c) for c in mid]
+            parts = []
+            for g in range(8):
+                cut = slice(8 * g, 8 * g + 8)
+                bottom = bmask[0, cut]
+                parts.append(fluxes(
+                    [adv[i, n, cut] for n in range(2)], [c[cut] for c in mid], [adv[i + 2, n, cut] for n in range(2)],
+                    [c[cut] for c in norths], [c[cut] for c in souths],
+                    jnp.where(bottom > kw, 0.25 * kx[i, cut], 0.0),
+                    bmask[3, cut] > kw, bmask[4, cut] > kw, bottom > kz,
+                ))
+            for n in range(2):
+                side = jnp.concatenate([part[1][n] for part in parts], axis=0)
+                flat[i, n] = jnp.concatenate([part[0][n] for part in parts], axis=0) + (north(side) - south(side))
+                vert[i, n] = jnp.concatenate([part[2][n] for part in parts], axis=0)
+
+    def flux_rest(step, carry):
+        flux_levels(2 + FB * step, FB)
+        return carry
+
+    def flux_ends(step, carry):
+        flux_levels(step * n_lev, 2)
+        return carry
+
+    lax.fori_loop(0, (n_lev - 2) // FB, flux_rest, 0)
 
     @pl.when(has_dn)
     def _():
@@ -388,81 +464,23 @@
     def _():
         z_copy.start()
 
-    def back_matrix(step, carry):
-        p_low, q_low = carry
-        at = n_lev - 1 - step
-        ratio = rdn[at]
-        p = pspk[at] + ratio * p_low
-        q = ratio * q_low
-        pspk[at] = p
-        qspk[at] = q
-        return p, q
-
-    lax.fori_loop(0, n_lev, back_matrix, (zero, one))
-
-    lax.fori_loop(2, n_lev - 2, transport_rest, 0)
-
-    @pl.when(inner)
-    def _():
-        z_copy.wait_recv()
-        z = zmat[...]
-        inv_t = 1.0 / (1.0 - z * send_end[o_end, o_end])
-        tmat[0] = inv_t
-        beta = z * send_end[i_end, o_end] * inv_t
-        tmat[1] = beta
-        qmat[...] = send_end[i_end, i_end] + send_end[o_end, i_end] * beta
-        q_copy.start()
-
-    def flux_level(at):
-        k = first + at - 1
-        kw = jnp.where(k < 0, FAR, k)
-        kz = jnp.where(k < 1, FAR, k + 1)
-        kappa = jnp.where(bmask[0] > kw, 0.25 * kx[at], 0.0)
-        f, w = fluxes(
-            [adv[at, n] for n in range(2)], [adv[at + 1, n] for n in range(2)],
-            [adv[at + 2, n] for n in range(2)], kappa,
-            bmask[3] > kw, bmask[4] > kw, bmask[0] > kz, plane_shifts(),
-        )
+
+    def pack_windows(at, count):
+        low = lanes((count, 8, LON)) % 16 < 8
         for n in range(2):
-            flat[at, n] = f[n]
-            vert[at, n] = w[n]
-
-    def flux_rest(step, carry):
-        flux_level(step)
-        return carry
-
-    def flux_ends(step, carry):
-        flux_level(jnp.where(step < 2, step, step + n_lev - 2))
-        return carry
-
-    lax.fori_loop(2, n_lev, flux_rest, 0)
-
-    @pl.when(has_dn)
-    def _():
-        ups[4].wait_recv()
-        ups[6].wait_recv()
-
-    @pl.when(has_up)
-    def _():
-        downs[4].wait_recv()
-        downs[5].wait_recv()
-
-    lax.fori_loop(0, 4, flux_ends, 0)
-
-    def pack_windows(step, carry):
-        at = step * chunk
-        low = lanes(shape) % 16 < 8
-        for n in range(2):
-            parts = [adv[pl.ds(at, chunk), n, 8 * g : 8 * g + 8, :] for g in range(8)]
-            gwin[n, pl.ds(at, chunk)] = jnp.where(low, pack(parts, 12), pack(parts, 4))
-        return carry
-
-    lax.fori_loop(0, (n_lev + 4) // chunk, pack_windows, 0)
+            parts = [adv[pl.ds(at, count), n, 8 * g : 8 * g + 8, :] for g in range(8)]
+            gwin[n, pl.ds(at, count)] = jnp.where(low, pack(parts, 12), pack(parts, 4))
+
+    def pack_own(step, carry):
+        pack_windows(2 + step * (n_lev // 2), n_lev // 2)
+        return carry
+
+    lax.fori_loop(0, 2, pack_own, 0)
 
     bot_r.wait_recv()
     bot_l.wait_recv()
-    lon_r.wait_recv()
-    lon_l.wait_recv()
+    for copy in lon_1:
+        copy.wait_recv()
 
     @pl.when(has_dn)
     def _():
@@ -488,6 +506,8 @@
         bstrip[3, side] = masks[3]
         bstrip[4, side] = masks[4]
 
+    chunk = (n_lev + 4) // 2
+    shape = (chunk, 8, LON)
     flatshape = (2 * chunk, 8, LON)
 
     def level_mask(which, start, floor, shift):
@@ -524,30 +544,86 @@
             awin[pl.ds(at, chunk), n, 1] = jnp.where(low, g, pltpu.roll(both[:, 1], 4, 2))
         return carry
 
-    lax.fori_loop(0, (n_lev + 4) // chunk, strip_transport, 0)
+    strip_transport(0, 0)
+    for copy in lon_2:
+        copy.wait_recv()
+    for i in range(2):
+        guest_l = guest_r = None
+        for j in range(3):
+            span = pl.ds(2 + j * guests, guests)
+            part_l = pltpu.roll(from_l[span, i], 2 + 2 * j, 2)
+            part_r = pltpu.roll(from_r[span, i], LON - 6 + 2 * j, 2)
+            guest_l = part_l if j == 0 else jnp.where(slot >= 2 + 2 * j, part_l, guest_l)
+            guest_r = part_r if j == 0 else jnp.where(slot >= 2 * j, part_r, guest_r)
+        from_l[pl.ds(2 + hosts, guests), i] = guest_l
+        from_r[pl.ds(2 + hosts, guests), i] = guest_r
+
+    strip_transport(1, 0)
+
+    @pl.when(has_dn)
+    def _():
+        ups[4].wait_recv()
+        ups[6].wait_recv()
+
+    @pl.when(has_up)
+    def _():
+        downs[4].wait_recv()
+        downs[5].wait_recv()
+
+    lax.fori_loop(0, 2, flux_ends, 0)
+
+    low2 = lanes((2, 8, LON)) % 16 < 8
+    for at in (0, n_lev + 2):
+        pack_windows(at, 2)
+        for n in range(2):
+            g = gwin[n, pl.ds(at, 2)]
+            awin[pl.ds(at, 2), n, 0] = jnp.where(low2, awin[pl.ds(at, 2), n, 0], g)
+            awin[pl.ds(at, 2), n, 1] = jnp.where(low2, g, awin[pl.ds(at, 2), n, 1])
+
+    @pl.when(inner)
+    def _():
+        z_copy.wait_recv()
+        z = zmat[...]
+        inv_t = 1.0 / (1.0 - z * send_end[o_end, o_end])
+        tmat[0] = inv_t
+        beta = z * send_end[i_end, o_end] * inv_t
+        tmat[1] = beta
+        qmat[...] = send_end[i_end, i_end] + send_end[o_end, i_end] * beta
+        q_copy.start()
+
+
+    chunk = FC
+    shape = (chunk, 8, LON)
+    flatshape = (2 * chunk, 8, LON)
 
     def strip_flux(step, carry):
         at = step * chunk
         k = first + at - 1
         wl = lanes(shape) % 16
         lb, rb = from_l[pl.ds(at + 1, chunk), 1], from_r[pl.ds(at + 1, chunk), 1]
-        kl = jnp.where(wl == 3, pltpu.roll(lb, LON - 5, 2), kown[pl.ds(at, chunk), 0])
-        kr = jnp.where(wl == 12, pltpu.roll(rb, 5, 2), kown[pl.ds(at, chunk), 1])
+        kl = jnp.where(wl == 3, pltpu.roll(lb, LON - 7, 2), kown[pl.ds(at, chunk), 0])
+        kr = jnp.where(wl == 12, pltpu.roll(rb, 7, 2), kown[pl.ds(at, chunk), 1])
         kappa = jnp.where(level_mask(2, k, 0, 0), 0.25 * join(kl, kr), 0.0)
 
         def window(shift):
             return [awin[pl.ds(at + shift, chunk), n].reshape(flatshape) for n in range(2)]
 
-        f, w = fluxes(
-            window(0), window(1), window(2), kappa,
-            level_mask(3, k, 0, 0), level_mask(4, k, 0, 0), level_mask(2, k, 1, 1), strip_shifts(),
+        _, _, north, south = strip_shifts()
+        mid = window(1)
+        f, y, w = fluxes(
+            window(0), mid, window(2), [north(c) for c in mid], [south(c) for c in mid], kappa,
+            level_mask(3, k, 0, 0), level_mask(4, k, 0, 0), level_mask(2, k, 1, 1),
         )
         for n in range(2):
-            sflat[pl.ds(at, chunk), n] = f[n].reshape(chunk, 2, 8, LON)
+            sflat[pl.ds(at, chunk), n] = (f[n] + (north(y[n]) - south(y[n]))).reshape(chunk, 2, 8, LON)
             svert[pl.ds(at, chunk), n] = w[n].reshape(chunk, 2, 8, LON)
         return carry
 
     lax.fori_loop(0, (n_lev + 4) // chunk, strip_flux, 0)
+
+    chunk = n_lev
+    shape = (chunk, 8, LON)
+    flatshape = (2 * chunk, 8, LON)
 
     def strip_update(step, carry):
         at = step * chunk
@@ -571,41 +647,62 @@
     lane = lanes(plane)
     on_edge = (lane < 6) | (lane >= LON - 6)
 
-    def way_down(at, carry):
-        wet = bmask[0] > first + at
-        scale, gain, prod = inv[at], gdn[at], rprod[at]
-        for n in range(2):
-            new = adv[at + 2, n] + jnp.where(wet, flat[at + 1, n] + vert[at + 2, n] - vert[at, n], 0.0)
-            packed = edge[at, n]
+    group = 4
+
+    def way_down(n, step, carry):
+        at = step * group
+        value, total = fval[at, n], yend[0, n]
+        for i in range(group):
+            here = at + i
+            wet = bmask[0] > first + here
+            new = adv[here + 2, n] + jnp.where(wet, flat[here + 1, n] + vert[here + 2, n] - vert[here, n], 0.0)
+            packed = edge[here, n]
             fixed = jnp.concatenate(
                 [pltpu.roll(packed, (LON - 8 - 16 * g) % LON, 1) for g in range(8)], axis=0
             )
             new = jnp.where(on_edge, fixed, new)
-            value = new * scale + gain * fval[at, n]
-            fval[at + 1, n] = value
-            yend[0, n] = yend[0, n] + prod * value
-        return carry
-
-    lax.fori_loop(0, n_lev, way_down, 0)
-    yend[1] = fval[n_lev]
-
-    z_val = remote(yend.at[i_end], zval, ZV, (lon, in_dev))
-    y_val = remote(yval, ypart, YV, (lon, 3 - dep))
-    x_val = remote(xout, xend.at[i_end], XO, (lon, out_dev))
+            value = new * inv[here] + gdn[here] * value
+            fval[here + 1, n] = value
+            total = total + rprod[here] * value
+        yend[0, n] = total
+        return carry
+
+    z_val = [remote(yend.at[i_end, n], zval.at[n], ZV + n, (lon, in_dev)) for n in range(2)]
+    y_val = [remote(yval.at[n], ypart.at[n], YV + n, (lon, 3 - dep)) for n in range(2)]
+    x_val = [remote(xout.at[n], xend.at[i_end, n], XO + n, (lon, out_dev)) for n in range(2)]
+
+    for n in range(2):
+        lax.fori_loop(0, n_lev // group, functools.partial(way_down, n), 0)
+        yend[1, n] = fval[n_lev, n]
+
+        @pl.when(outer)
+        def _():
+            z_val[n].start()
 
     @pl.when(outer)
     def _():
-        z_val.start()
         xend[o_end] = jnp.zeros((2,) + plane, jnp.float32)
 
     @pl.when(inner)
     def _():
-        z_val.wait_recv()
         for n in range(2):
+            z_val[n].wait_recv()
             alpha = (zval[n] + zmat[...] * yend[o_end, n]) * tmat[0]
             xend[o_end, n] = alpha
             yval[n] = yend[i_end, n] + send_end[o_end, i_end] * alpha
-        y_val.start()
+            y_val[n].start()
+
+    def back_matrix(step, carry):
+        p_low, q_low = carry
+        at = n_lev - 1 - step
+        ratio = rdn[at]
+        p = pspk[at] + ratio * p_low
+        q = ratio * q_low
+        pspk[at] = p
+        qspk[at] = q
+        return p, q
+
+    lax.fori_loop(0, n_lev, back_matrix, (zero, one))
 
     def way_up(step, carry):
         at = n_lev - 1 - step
@@ -619,38 +716,32 @@
     @pl.when(inner)
     def _():
         q_copy.wait_recv()
-        y_val.wait_recv()
         q_other = qpart[...]
         inv_m = 1.0 / (1.0 - q_other * qmat[...])
-        oo, io = send_end[o_end, o_end], send_end[i_end, o_end]
         for n in range(2):
+            y_val[n].wait_recv()
             x_in = (ypart[n] + q_other * yval[n]) * inv_m
-            xout[n] = (yend[o_end, n] + oo * zval[n] + io * x_in) * tmat[0]
+            xout[n] = (yend[o_end, n] + send_end[o_end, o_end] * zval[n] + send_end[i_end, o_end] * x_in) * tmat[0]
+            x_val[n].start()
             xend[i_end, n] = x_in
-        x_val.start()
-        for n in range(2):
-            xend[o_end, n] = xend[o_end, n] + tmat[1] * xend[i_end, n]
+            xend[o_end, n] = xend[o_end, n] + tmat[1] * x_in
 
     @pl.when(outer)
     def _():
-        x_val.wait_recv()
-
-    stores = []
+        for copy in x_val:
+            copy.wait_recv()
+
     part = n_lev // 4
     for i in range(4):
         def finish(at, carry):
             p, q = pspk[at], qspk[at]
             for n in range(2):
-                obuf[n, at] = fval[at + 1, n] + p * xend[0, n] + q * xend[1, n]
+                out_hbm[n, at] = fval[at + 1, n] + p * xend[0, n] + q * xend[1, n]
             return carry
 
         lax.fori_loop(i * part, (i + 1) * part, finish, 0)
-        span = pl.ds(i * part, part)
-        copy = pltpu.make_async_copy(obuf.at[:, span], out_hbm.at[:, span], out_sem.at[i])
-        copy.start()
-        stores.append(copy)
-
-    for copy in (lon_r, lon_l, bot_r, bot_l):
+
+    for copy in lon_1 + lon_2 + [bot_r, bot_l]:
         copy.wait_send()
 
     @pl.when(has_up)
@@ -666,16 +757,14 @@
     @pl.when(outer)
     def _():
         z_copy.wait_send()
-        z_val.wait_send()
+        for copy in z_val:
+            copy.wait_send()
 
     @pl.when(inner)
     def _():
         q_copy.wait_send()
-        y_val.wait_send()
-        x_val.wait_send()
-
-    for copy in stores:
-        copy.wait()
+        for copy in y_val + x_val:
+            copy.wait_send()
 
 
 def per_device(n_lon, n_dep, tracers, u_east, v_north, kappa_h, kappa_v, bottom):
@@ -705,22 +794,21 @@
         f32(LAT, LON), f32(LAT, LON), f32(LAT, LON),
         f32(2, LAT, LON), f32(2, LAT, LON), f32(2, LAT, LON), f32(2, LAT, LON),
         f32(2, 2, LAT, LON), f32(2, LAT, LON),
-        f32(2, n_lev, LAT, LON),
-        pltpu.SemaphoreType.DMA((6,)), pltpu.SemaphoreType.DMA((4,)),
+        pltpu.SemaphoreType.DMA((4 * NQ + 2,)),
         pltpu.SemaphoreType.DMA((N_COPIES,)), pltpu.SemaphoreType.DMA((N_COPIES,)),
     ]
-    hbm = pl.BlockSpec(memory_space=pl.ANY)
+    hbm = pl.BlockSpec(memory_space=pltpu.HBM)
     return pl.pallas_call(
         functools.partial(kernel, n_lon, n_dep, n_lev),
         out_shape=jax.ShapeDtypeStruct(tracers.shape, jnp.float32),
         in_specs=[hbm] * 6,
-        out_specs=hbm,
+        out_specs=pl.BlockSpec(memory_space=pltpu.VMEM),
         scratch_shapes=scratch,
         name="tracer_step",
         compiler_params=pltpu.CompilerParams(
             collective_id=0, has_side_effects=True, vmem_limit_bytes=48 << 20
         ),
-    )(tracers, u_east, v_north, kappa_h, kappa_v, bottom)
+    )(*(pltpu.with_memory_space_constraint(a, pltpu.HBM) for a in (tracers, u_east, v_north, kappa_h, kappa_v, bottom)))
 
 
 def solution(mesh):

time: 48 us -> 29.3 us (0.61)
  the two profiles are of different devices: /device:TPU:65 before, /device:TPU:1 now
where the time goes in v3:
time: 29.3 us; the launch traced here: 29.2 us
  Pallas kernels  28.1 us (96%)
  local copies, waits for them, and re-layouts  1.06 us (4%)
    pallas_call x1, Pallas kernels, per_device(): pl.pallas_call(functools.partial(kernel, n_lon, n_dep, n_lev), out_shape=...  28.1 us
    unnamed x1, local copies, waits for them, and re-layouts  1.06 us

profile of v3, /device:TPU:1, one launch (start us, length us, event | category | flops | bytes accessed | tf_op | source)
XLA Modules:
  0.0 29.2 jit_solution(12797616001285142961)
XLA Ops:
  0.0 28.1 %tracer_step.1 = f32[2,20,64,128]{3,2,1,0:T(8,128)S(1)} custom-call(f32[2,20,64,128]{3,2,1,0:T(8,128)} %tr_hbm.1, f32[20,64,128]{2,1,0:T(8,128)} %u_hbm.1, f32[20,64,128]{2,1,0:T(8,128)} %v_hbm.1, f32[20,64,128]{2,1,0:T(8,128)} %kh_hbm.1, f32[20,64,128]{2,1,0:T(8,128)} %kv_hbm.1, s32[64,128]{1,0:T(8,128)} %bot_hbm.1), custom_call_target="tpu_custom_call" | custom-call | tf_op jit(solution)/shard_map/tracer_step/pallas_call | solution.py:801
  28.2 1.1 %copy.8 = f32[2,20,64,128]{3,2,1,0:T(8,128)} copy(f32[2,20,64,128]{3,2,1,0:T(8,128)S(1)} %tracer_step.1) | data formatting | bytes 2621440

commit v4 on v3

--- a/solution.py
+++ b/solution.py
@@ -14,7 +14,7 @@
 THERMAL = 0.2
 HALINE = 0.8
 FAR = 1 << 20
-TB, FB, FC, NQ = 8, 2, 12, 2
+TB, FB, FC, NQ = 4, 2, 12, 2
 
 (LON_R, LON_L, BOT_R, BOT_L, DG_RU, DG_RD, DG_LU, DG_LD, E_U, E_D, K_U, K_D, KX_U, KX_D, KV_U, ADV_U, ADV_D, ZM, QM) = range(19)
 ZV, YV, XO, LON2 = 19, 21, 23, 25
@@ -647,7 +647,7 @@
     lane = lanes(plane)
     on_edge = (lane < 6) | (lane >= LON - 6)
 
-    group = 4
+    group = 10
 
     def way_down(n, step, carry):
         at = step * group

time: 29.3 us -> 28.8 us (0.983)
  Pallas kernels: 28.1 us -> 27.7 us
    pallas_call x1, Pallas kernels: 28.1 us -> 27.7 us  [per_device(): pl.pallas_call(functools.partial(kernel, n_lon, n_dep, n_lev), out_shape=...]
where the time goes in v4:
time: 28.8 us; the launch traced here: 28.7 us
  Pallas kernels  27.7 us (96%)
  local copies, waits for them, and re-layouts  1.06 us (4%)
    pallas_call x1, Pallas kernels, per_device(): pl.pallas_call(functools.partial(kernel, n_lon, n_dep, n_lev), out_shape=...  27.7 us
    unnamed x1, local copies, waits for them, and re-layouts  1.06 us

profile of v4, /device:TPU:1, one launch (start us, length us, event | category | flops | bytes accessed | tf_op | source)
XLA Modules:
  0.0 28.7 jit_solution(11335703978320402754)
XLA Ops:
  0.0 27.7 %tracer_step.1 = f32[2,20,64,128]{3,2,1,0:T(8,128)S(1)} custom-call(f32[2,20,64,128]{3,2,1,0:T(8,128)} %tr_hbm.1, f32[20,64,128]{2,1,0:T(8,128)} %u_hbm.1, f32[20,64,128]{2,1,0:T(8,128)} %v_hbm.1, f32[20,64,128]{2,1,0:T(8,128)} %kh_hbm.1, f32[20,64,128]{2,1,0:T(8,128)} %kv_hbm.1, s32[64,128]{1,0:T(8,128)} %bot_hbm.1), custom_call_target="tpu_custom_call" | custom-call | tf_op jit(solution)/shard_map/tracer_step/pallas_call | solution.py:801
  27.7 1.1 %copy.8 = f32[2,20,64,128]{3,2,1,0:T(8,128)} copy(f32[2,20,64,128]{3,2,1,0:T(8,128)S(1)} %tracer_step.1) | data formatting | bytes 2621440
